TPU v7x, 32 devices: a whole 2x2x4 slice. The times are simulated.
32 devices in a mesh: layer: 4 (over x, core), lat: 8 (over z, y).
Axes of the slice: x: 2, y: 2, z: 4, core: 2. Of those that a mesh axis runs over, the one named last changes fastest.
Arguments:
- resid_in: bfloat16 [4, 4096, 256], P('layer', 'lat'), may hold values from -6 to 6
- resid_out: bfloat16 [4, 4096, 256], P('layer', 'lat'), may hold values from -80 to 80
- token_ids: int32 [256], replicated, may hold values from 0 to 128255, as said below
- active_mask: int32 [4, 6144, 256], P('layer', 'lat'), may hold values 0 or 1
- enc_weight: bfloat16 [4, 6144, 4096], P('layer', 'lat'), may hold values from -0.09375 to 0.09375
- enc_bias: bfloat16 [4, 6144], P('layer', 'lat'), may hold values from -3 to 3
- dec_weight: bfloat16 [4, 4, 6144, 4096], P('layer', None, 'lat'), may hold values from -0.078125 to 0.078125
- dec_bias: bfloat16 [4, 4096], P('layer', 'lat'), may hold values from -3 to 3
Outputs:
- enc_grad: bfloat16 [4, 6144, 4096], P('layer', 'lat')
- dec_grad: bfloat16 [4, 4, 6144, 4096], P('layer', None, 'lat')
- total_loss: float32 [], replicated
Inputs may be any that keep to these rules, and one draw needn't show every extreme that they name: `token_ids`: ids of the Llama 3 vocabulary; the begin-of-text id 128000 stands at position 0 and at scattered other positions.
All inputs are finite; a program needn't handle non-finite values. No bound on the sum of `active_mask` on one device may be relied on, other than what follows from the above.
Results may differ from a plain program's by a relative error of at most 0.007.
Values may be sent and summed in bfloat16 or wider, within the bound.
A program may use at most 128 MiB of HBM per device.

v0:
```python
import jax
import jax.numpy as jnp
from jax import lax
from jax.sharding import PartitionSpec as P

EPSILON = 1e-05


def on_device(
    resid_in, resid_out, token_ids, active_mask, enc_weight, enc_bias, dec_weight, dec_bias
):
    layer_count = lax.axis_size("layer")
    layer_here = lax.axis_index("layer")
    inputs_local = resid_in[0]
    weight_enc = enc_weight[0]
    lat_rows = weight_enc.shape[0]
    feature_count = weight_enc.shape[1]
    token_count = inputs_local.shape[1]
    whole_inputs = lax.all_gather(inputs_local, "lat", axis=0, tiled=True)
    preact = jnp.dot(weight_enc, whole_inputs, preferred_element_type=jnp.float32)
    preact = preact + enc_bias[0].astype(jnp.float32)[:, None]
    gating = active_mask[0].astype(jnp.float32)
    latents = (gating * preact).astype(jnp.bfloat16)
    source_ids = jnp.arange(layer_count)
    gathered = lax.all_gather(latents[None], "layer", axis=0, tiled=True)
    acts_stack = jnp.where(
        (source_ids <= layer_here)[:, None, None], gathered, jnp.zeros((), jnp.bfloat16)
    )
    stack_rows = acts_stack.reshape(layer_count * lat_rows, token_count)
    weight_rows = dec_weight[0].reshape(layer_count * lat_rows, feature_count)
    kept_tokens = (token_ids != 128000).astype(jnp.float32)
    total_cells = feature_count * token_count
    wanted = resid_out[0].astype(jnp.float32)
    recon = lax.psum_scatter(
        lax.dot_general(
            weight_rows, stack_rows, (((0,), (0,)), ((), ())), preferred_element_type=jnp.float32
        ),
        "lat",
        scatter_dimension=0,
        tiled=True,
    )
    recon = recon + dec_bias[0].astype(jnp.float32)[:, None]
    centered = wanted - jnp.mean(wanted, axis=1, keepdims=True)
    residual_err = kept_tokens[None, :] * (recon - wanted)
    squares_err, squares_tgt = lax.psum(
        (jnp.sum(residual_err * residual_err), jnp.sum(centered * centered)), "lat"
    )
    spread = squares_tgt / total_cells + EPSILON
    layer_loss = squares_err / (2.0 * spread * total_cells)
    total_loss = lax.psum(layer_loss, "layer")
    out_grad = (residual_err / spread).astype(jnp.bfloat16)
    full_grad = lax.all_gather(out_grad, "lat", axis=0, tiled=True)
    grad_rows = jnp.dot(weight_rows, full_grad, preferred_element_type=jnp.float32).reshape(
        layer_count, lat_rows, token_count
    )
    grad_rows = grad_rows * (source_ids <= layer_here).astype(jnp.float32)[:, None, None]
    dec_out = lax.dot_general(
        stack_rows, full_grad, (((1,), (1,)), ((), ())), preferred_element_type=jnp.float32
    )
    dec_out = dec_out.astype(jnp.bfloat16).reshape(1, layer_count, lat_rows, feature_count)
    latent_grad = lax.psum_scatter(grad_rows, "layer", scatter_dimension=0, tiled=True)[0]
    preact_grad = (gating * latent_grad).astype(jnp.bfloat16)
    enc_out = lax.dot_general(
        preact_grad, whole_inputs, (((1,), (1,)), ((), ())), preferred_element_type=jnp.float32
    )
    return (enc_out.astype(jnp.bfloat16)[None], dec_out, total_loss)


def solution(mesh):
    in_specs = (
        P("layer", "lat", None),
        P("layer", "lat", None),
        P(),
        P("layer", "lat", None),
        P("layer", "lat", None),
        P("layer", "lat"),
        P("layer", None, "lat", None),
        P("layer", "lat"),
    )
    out_specs = (P("layer", "lat", None), P("layer", None, "lat", None), P())
    return jax.shard_map(
        on_device, mesh=mesh, in_specs=in_specs, out_specs=out_specs, check_vma=False
    )
```

profile of v0, /device:TPU:0, one launch (start us, length us, event | category | flops | bytes accessed | tf_op | source)
XLA Modules:
  0.0 334.2 jit_solution(15536479008416231452)
XLA Ops:
  7.2 0.0 all-gather.8.cloned.1.call-start
  7.2 0.7 all-gather.8.cloned.1.call-update
  7.9 0.0 all-gather.10.cloned.1.call-start
  7.9 0.7 convert_reduce_fusion.1
  8.6 53.5 %all-gather.8.cloned.1.call-done = bf16[1,4096,256]{2,1,0:T(8,128)(2,1)} async-done(((bf16[1,512,256]{2,1,0:T(8,128)(2,1)}), bf16[1,4096,256]{2,1,0:T(8,128)(2,1)}) %all-gather.8.cloned.1.call-update) | async-done | bytes 2097168 | tf_op jit(solution)/shard_map/all_gather | solution.py:19
  62.2 6.1 %fusion.15 = bf16[768,256]{1,0:T(8,128)(2,1)} fusion(bf16[1,4096,256]{2,1,0:T(8,128)(2,1)} %all-gather.8.cloned.1.call-done, bf16[1,768,4096]{2,1,0:T(8,128)(2,1)} %param.12, s32[1,768,256]{2,1,0:T(8,128)} %param.11, f32[768]{0:T(1024)S(1)} %convert_reduce_fusion.1), kind=kOutput, calls=%fused_computation.13 | convolution fusion | flops 1611399168 | bytes 9571328 | tf_op jit(solution)/shard_map/dot_general | solution.py:20
  68.2 0.0 all-gather.10.cloned.1.call-update
  68.3 0.0 reduce-scatter.3.cloned.1.call-start
  68.3 18.2 %all-gather.10.cloned.1.call-done = bf16[3072,256]{1,0:T(8,128)(2,1)} async-done(((bf16[768,256]{1,0:T(8,128)(2,1)}), bf16[3072,256]{1,0:T(8,128)(2,1)}) %all-gather.10.cloned.1.call-update) | async-done | bytes 1572880 | tf_op jit(solution)/shard_map/all_gather | solution.py:25
  86.6 1.6 broadcast_select_fusion
  88.2 13.7 %convolution_bitcast_fusion = f32[4096,256]{0,1:T(8,128)} fusion(bf16[3072,256]{1,0:T(8,128)(2,1)S(1)} %bitcast.66, bf16[3072,4096]{1,0:T(8,128)(2,1)} %bitcast.64), kind=kOutput, calls=%fused_computation.5 | convolution fusion | flops 6442450944 | bytes 30932992 | tf_op jit(solution)/shard_map/dot_general | solution.py:35
  101.8 0.0 copy-start.1
  101.8 0.0 copy-start.2
  101.8 0.0 copy-start.3
  101.8 0.0 reduce-scatter.3.cloned.1.call-update
  101.8 0.0 all-gather.6.cloned.1.call-start
  101.9 0.9 copy-done.1
  102.8 0.1 copy.11
  102.9 0.0 copy-done.2
  102.9 0.1 convert_reduce_fusion
  103.0 0.0 copy-done.3
  103.0 87.4 %reduce-scatter.3.cloned.1.call-done = f32[512,256]{0,1:T(8,128)} async-done(((f32[4096,256]{0,1:T(8,128)}), f32[512,256]{0,1:T(8,128)}) %reduce-scatter.3.cloned.1.call-update) | async-done | bytes 524304 | tf_op jit(solution)/shard_map/reduce_scatter | solution.py:34
  190.5 1.9 multiply_reduce_fusion
  192.4 20.8 %all-reduce = (f32[]{:T(128)}, f32[]{:T(128)}) all-reduce(f32[]{:T(128)} %get-tuple-element.4, f32[]{:T(128)} %get-tuple-element.3), channel_id=1, replica_groups=mesh['layer'=4,'lat'=8] {'lat'}, use_global_device_ids=true, to_apply=%region_3.4 | all-reduce | flops 2 | bytes 16 | tf_op jit(solution)/shard_map/psum | solution.py:45
  213.8 1.9 divide_convert_fusion
  215.7 0.0 all-gather.6.cloned.1.call-update
  215.7 0.0 reduce-scatter.5.cloned.1.call-start
  215.8 48.4 %all-gather.6.cloned.1.call-done = bf16[4096,256]{0,1:T(8,128)(2,1)} async-done(((bf16[512,256]{0,1:T(8,128)(2,1)}), bf16[4096,256]{0,1:T(8,128)(2,1)}) %all-gather.6.cloned.1.call-update) | async-done | bytes 2097168 | tf_op jit(solution)/shard_map/all_gather | solution.py:52
  264.2 13.3 %convolution_bitcast_fusion.1 = f32[3072,256]{0,1:T(8,128)} fusion(bf16[4096,256]{0,1:T(8,128)(2,1)} %all-gather.6.cloned.1.call-done, bf16[3072,4096]{1,0:T(8,128)(2,1)} %bitcast.65), kind=kOutput, calls=%fused_computation.6 | convolution fusion | flops 6442450944 | bytes 30408704 | tf_op jit(solution)/shard_map/dot_general | solution.py:53
  277.5 3.5 %copy.12 = f32[3072,256]{1,0:T(8,128)} copy(f32[3072,256]{0,1:T(8,128)} %convolution_bitcast_fusion.1) | data formatting | bytes 6291456 | tf_op jit(solution)/shard_map/dot_general | solution.py:53
  281.1 3.9 %broadcast_multiply_fusion = f32[4,768,256]{2,1,0:T(8,128)} fusion(f32[4,768,256]{2,1,0:T(8,128)} %bitcast.68, f32[4]{0:T(128)S(1)} %fusion.27), kind=kLoop, calls=%fused_computation.9 | loop fusion | flops 786432 | bytes 6291472 | tf_op jit(solution)/shard_map/mul | solution.py:56
  285.0 0.0 reduce-scatter.5.cloned.1.call-update
  285.7 6.8 %psum.23 = f32[]{:T(128)} all-reduce(f32[]{:T(128)S(6)} %div.23), channel_id=1, replica_groups=mesh['layer'=4,'lat'=8] {'layer'}, use_global_device_ids=true, to_apply=%region_7.8 | all-reduce | flops 1 | bytes 8 | tf_op jit(solution)/shard_map/psum | solution.py:50
  292.5 0.0 copy-start
  292.5 14.1 %convolution_convert_fusion = bf16[3072,4096]{1,0:T(8,128)(2,1)} fusion(bf16[3072,256]{1,0:T(8,128)(2,1)S(1)} %bitcast.67, bf16[4096,256]{0,1:T(8,128)(2,1)} %all-gather.6.cloned.1.call-done), kind=kOutput, calls=%fused_computation | convolution fusion | flops 6455033856 | bytes 28835840 | tf_op jit(solution)/shard_map/dot_general | solution.py:57
  306.6 14.6 %reduce-scatter.5.cloned.1.call-done = f32[1,768,256]{2,1,0:T(8,128)} async-done(((f32[4,768,256]{2,1,0:T(8,128)}), f32[1,768,256]{2,1,0:T(8,128)}) %reduce-scatter.5.cloned.1.call-update) | async-done | bytes 786448 | tf_op jit(solution)/shard_map/reduce_scatter | solution.py:61
  321.3 0.0 copy-done
  321.3 6.4 %fusion.2 = bf16[1,768,4096]{2,1,0:T(8,128)(2,1)} fusion(bf16[1,4096,256]{2,1,0:T(8,128)(2,1)} %all-gather.8.cloned.1.call-done, f32[1,768,256]{2,1,0:T(8,128)} %reduce-scatter.5.cloned.1.call-done, s32[1,768,256]{2,1,0:T(8,128)S(1)} %copy-done), kind=kOutput, calls=%fused_computation.4 | convolution fusion | flops 1614348288 | bytes 9961472 | tf_op jit(solution)/shard_map/dot_general | solution.py:63
  (5 shorter events, 0.0 us)
Async XLA Ops:
  7.2 55.0 %all-gather.8.cloned.1.call-start = ((), (), s32[]{:S(2)}) async-start(), calls=%async_computation.5 | async-start | bytes 2359296 | tf_op jit(solution)/shard_map/all_gather | solution.py:19
  7.9 78.7 %all-gather.10.cloned.1.call-start = ((), (), s32[]{:S(2)}) async-start(), calls=%async_computation.6 | async-start | bytes 1966080 | tf_op jit(solution)/shard_map/all_gather | solution.py:25
  68.3 122.2 %reduce-scatter.3.cloned.1.call-start = ((), (), s32[]{:S(2)}) async-start(), calls=%async_computation.2 | async-start | bytes 4718592 | tf_op jit(solution)/shard_map/reduce_scatter | solution.py:34
  101.8 0.9 copy-start.1
  101.8 1.1 copy-start.2
  101.8 1.2 copy-start.3
  101.8 162.3 %all-gather.6.cloned.1.call-start = ((), (), s32[]{:S(2)}) async-start(), calls=%async_computation.3 | async-start | bytes 2359296 | tf_op jit(solution)/shard_map/all_gather | solution.py:52
  215.7 105.6 %reduce-scatter.5.cloned.1.call-start = ((), (), s32[]{:S(2)}) async-start(), calls=%async_computation.4 | async-start | bytes 3932160 | tf_op jit(solution)/shard_map/reduce_scatter | solution.py:61
  292.5 28.8 %copy-start = (s32[1,768,256]{2,1,0:T(8,128)S(1)}, s32[1,768,256]{2,1,0:T(8,128)}, u32[]{:S(2)}) copy-start(s32[1,768,256]{2,1,0:T(8,128)} %param.11) | copy-start | bytes 2359300
Sparse Core Ops, SparseCore 0:
  10.1 51.9 all-gather.7
  68.4 18.1 all-gather.9
  102.0 88.4 reduce-scatter.2
  215.8 48.3 all-gather.5
  285.1 36.1 reduce-scatter.4
where the time goes:
time: 335 us; the launch traced here: 334 us
  waiting for transfers between devices  223 us (67%)
  matrix products  53.6 us (16%)
  blocking collectives  27.6 us (8%)
  between operations  15.2 us (5%)
  other arithmetic  10 us (3%)
  local copies, waits for them, and re-layouts  4.56 us (1%)
    reduce_scatter x1, waiting for transfers between devices, on_device(): lax.psum_scatter(lax.dot_general(weight_rows, stack_rows, (((0,), (0,)),...  87.4 us
    all_gather x1, waiting for transfers between devices, on_device(): whole_inputs = lax.all_gather(inputs_local, 'lat', axis=0, tiled=True)  53.5 us
    all_gather x1, waiting for transfers between devices, on_device(): full_grad = lax.all_gather(out_grad, 'lat', axis=0, tiled=True)  48.4 us
    psum x1, blocking collectives, on_device(): lax.psum((jnp.sum(residual_err * residual_err), jnp.sum(centered * center...  20.8 us
    all_gather x1, waiting for transfers between devices, on_device(): gathered = lax.all_gather(latents[None], 'layer', axis=0, tiled=True)  18.2 us
    reduce_scatter x1, waiting for transfers between devices, on_device(): lax.psum_scatter(grad_rows, 'layer', scatter_dimension=0, tiled=True)[0]  14.6 us
    dot_general x1, matrix products, on_device(): lax.dot_general(stack_rows, full_grad, (((1,), (1,)), ((), ())), preferre...  14.1 us
    dot_general x1, matrix products, on_device(): lax.dot_general(weight_rows, stack_rows, (((0,), (0,)), ((), ())), prefer...  13.7 us
  transfers between devices with their start and end apart: 5, of which 5 were waited for; matrix products, arithmetic and copies ran while one was open for 5% of the time, Pallas kernels for 0%

commit v1 on v0

--- a/solution.py
+++ b/solution.py
@@ -9,6 +9,22 @@
 def on_device(
     resid_in, resid_out, token_ids, active_mask, enc_weight, enc_bias, dec_weight, dec_bias
 ):
+
+    def prepare_array(vals, axis_key):
+        n_all = jax.lax.axis_size(axis_key)
+        bank = []
+        for to_i in range(n_all):
+            bank.append((to_i, (to_i + 1) % n_all))
+        extra = [None] * n_all
+        extra[n_all - 1] = vals
+        for d in range(n_all - 2, -1, -1):
+            extra[d] = jax.lax.ppermute(extra[d + 1], axis_name=axis_key, perm=bank)
+        high = jnp.concatenate(extra, axis=0)
+        out_arr = jax.lax.axis_index(axis_key)
+        clean = (out_arr + 1) * vals.shape[0]
+        block_out = jnp.roll(high, shift=clean, axis=0)
+        return block_out
+
     layer_count = lax.axis_size("layer")
     layer_here = lax.axis_index("layer")
     inputs_local = resid_in[0]
@@ -16,7 +32,7 @@
     lat_rows = weight_enc.shape[0]
     feature_count = weight_enc.shape[1]
     token_count = inputs_local.shape[1]
-    whole_inputs = lax.all_gather(inputs_local, "lat", axis=0, tiled=True)
+    whole_inputs = prepare_array(inputs_local, "lat")
     preact = jnp.dot(weight_enc, whole_inputs, preferred_element_type=jnp.float32)
     preact = preact + enc_bias[0].astype(jnp.float32)[:, None]
     gating = active_mask[0].astype(jnp.float32)

time: 335 us -> 349 us (1.042)
  local copies, waits for them, and re-layouts: 4.56 us -> 14.1 us
  waiting for transfers between devices: 223 us -> 231 us
  matrix products: 53.6 us -> 49.1 us
    ppermute x0 -> x7, waiting for transfers between devices: none -> 63.7 us  [prepare_array(): extra[d] = jax.lax.ppermute(extra[d + 1], axis_name=axis_key, perm=bank)]
    all_gather x1 -> x0, waiting for transfers between devices: 53.5 us -> none  [on_device(): whole_inputs = lax.all_gather(inputs_local, 'lat', axis=0, tiled=True)]
    unnamed x9 -> x38, local copies, waits for them, and re-layouts: 1.02 us -> 6.09 us
  transfers between devices with their start and end apart: 5 -> 11, of which waited for: 5 -> 11; matrix products, arithmetic and copies ran while one was open for 5% -> 5% of each run, Pallas kernels for 0% -> 0%
where the time goes in v1:
time: 349 us; the launch traced here: 348 us
  waiting for transfers between devices  231 us (66%)
  matrix products  49.1 us (14%)
  blocking collectives  27.5 us (8%)
  between operations  15.5 us (4%)
  local copies, waits for them, and re-layouts  14.1 us (4%)
  other arithmetic  7.31 us (2%)
    reduce_scatter x1, waiting for transfers between devices, on_device(): lax.psum_scatter(lax.dot_general(weight_rows, stack_rows, (((0,), (0,)),...  87.5 us
    ppermute x7, waiting for transfers between devices, prepare_array(): extra[d] = jax.lax.ppermute(extra[d + 1], axis_name=axis_key, perm=bank)  63.7 us
    all_gather x1, waiting for transfers between devices, on_device(): full_grad = lax.all_gather(out_grad, 'lat', axis=0, tiled=True)  48.2 us
    psum x1, blocking collectives, on_device(): lax.psum((jnp.sum(residual_err * residual_err), jnp.sum(centered * center...  20.8 us
    all_gather x1, waiting for transfers between devices, on_device(): gathered = lax.all_gather(latents[None], 'layer', axis=0, tiled=True)  17.1 us
    reduce_scatter x1, waiting for transfers between devices, on_device(): lax.psum_scatter(grad_rows, 'layer', scatter_dimension=0, tiled=True)[0]  14.7 us
    dot_general x1, matrix products, on_device(): lax.dot_general(stack_rows, full_grad, (((1,), (1,)), ((), ())), preferre...  14.2 us
    dot_general x1, matrix products, on_device(): lax.dot_general(weight_rows, stack_rows, (((0,), (0,)), ((), ())), prefer...  13.6 us
  transfers between devices with their start and end apart: 11, of which 11 were waited for; matrix products, arithmetic and copies ran while one was open for 5% of the time, Pallas kernels for 0%

profile of v1, /device:TPU:0, one launch (start us, length us, event | category | flops | bytes accessed | tf_op | source)
XLA Modules:
  0.0 348.0 jit_solution(655161006146315568)
XLA Ops:
  7.2 0.0 all-gather.6.cloned.1.call-start
  7.2 3.0 collective-permute-start
  10.2 9.6 %collective-permute-done = bf16[512,256]{1,0:T(8,128)(2,1)S(1)} collective-permute-done((bf16[512,256]{1,0:T(8,128)(2,1)}, bf16[512,256]{1,0:T(8,128)(2,1)S(1)}, u32[]{:S(2)}, u32[]{:S(2)}) %collective-permute-start) | collective-permute-done | bytes 262176 | tf_op jit(solution)/shard_map/ppermute | solution.py:21
  19.8 0.0 collective-permute-start.1
  19.8 10.2 %collective-permute-done.1 = bf16[512,256]{1,0:T(8,128)(2,1)S(1)} collective-permute-done((bf16[512,256]{1,0:T(8,128)(2,1)S(1)}, bf16[512,256]{1,0:T(8,128)(2,1)S(1)}, u32[]{:S(2)}, u32[]{:S(2)}) %collective-permute-start.1) | collective-permute-done | bytes 262176 | tf_op jit(solution)/shard_map/ppermute | solution.py:21
  30.0 9.3 %collective-permute-done.2 = bf16[512,256]{1,0:T(8,128)(2,1)S(1)} collective-permute-done((bf16[512,256]{1,0:T(8,128)(2,1)S(1)}, bf16[512,256]{1,0:T(8,128)(2,1)S(1)}, u32[]{:S(2)}, u32[]{:S(2)}) %collective-permute-start.2) | collective-permute-done | bytes 262176 | tf_op jit(solution)/shard_map/ppermute | solution.py:21
  39.3 9.1 %collective-permute-done.3 = bf16[512,256]{1,0:T(8,128)(2,1)S(1)} collective-permute-done((bf16[512,256]{1,0:T(8,128)(2,1)S(1)}, bf16[512,256]{1,0:T(8,128)(2,1)S(1)}, u32[]{:S(2)}, u32[]{:S(2)}) %collective-permute-start.3) | collective-permute-done | bytes 262176 | tf_op jit(solution)/shard_map/ppermute | solution.py:21
  48.3 0.0 collective-permute-start.4
  48.3 9.1 %collective-permute-done.4 = bf16[512,256]{1,0:T(8,128)(2,1)S(1)} collective-permute-done((bf16[512,256]{1,0:T(8,128)(2,1)S(1)}, bf16[512,256]{1,0:T(8,128)(2,1)S(1)}, u32[]{:S(2)}, u32[]{:S(2)}) %collective-permute-start.4) | collective-permute-done | bytes 262176 | tf_op jit(solution)/shard_map/ppermute | solution.py:21
  57.4 0.0 collective-permute-start.5
  57.4 9.7 %collective-permute-done.5 = bf16[512,256]{1,0:T(8,128)(2,1)S(1)} collective-permute-done((bf16[512,256]{1,0:T(8,128)(2,1)S(1)}, bf16[512,256]{1,0:T(8,128)(2,1)S(1)}, u32[]{:S(2)}, u32[]{:S(2)}) %collective-permute-start.5) | collective-permute-done | bytes 262176 | tf_op jit(solution)/shard_map/ppermute | solution.py:21
  67.1 1.4 copy.13
  68.5 0.7 convert_reduce_fusion.1
  69.3 0.0 copy-start.9
  69.3 6.9 %collective-permute-done.6 = bf16[512,256]{1,0:T(8,128)(2,1)S(1)} collective-permute-done((bf16[512,256]{1,0:T(8,128)(2,1)S(1)}, bf16[512,256]{1,0:T(8,128)(2,1)S(1)}, u32[]{:S(2)}, u32[]{:S(2)}) %collective-permute-start.6) | collective-permute-done | bytes 262176 | tf_op jit(solution)/shard_map/ppermute | solution.py:21
  76.6 1.9 copy-done.4
  78.6 2.6 fusion.20
  81.2 0.0 all-gather.6.cloned.1.call-update
  81.3 0.0 reduce-scatter.3.cloned.1.call-start
  81.3 17.1 %all-gather.6.cloned.1.call-done = bf16[3072,256]{0,1:T(8,128)(2,1)} async-done(((bf16[768,256]{0,1:T(8,128)(2,1)}), bf16[3072,256]{0,1:T(8,128)(2,1)}) %all-gather.6.cloned.1.call-update) | async-done | bytes 1572880 | tf_op jit(solution)/shard_map/all_gather | solution.py:41
  98.4 3.3 reshape.48
  101.7 0.7 broadcast_select_fusion
  102.4 0.3 copy.17
  102.7 0.0 copy-start
  102.7 1.1 copy-done
  103.8 13.6 %convolution_bitcast_fusion = f32[4096,256]{0,1:T(8,128)} fusion(bf16[3072,256]{0,1:T(8,128)(2,1)S(1)} %bitcast.69, bf16[3072,4096]{1,0:T(8,128)(2,1)} %bitcast.75), kind=kOutput, calls=%fused_computation.5 | convolution fusion | flops 6442450944 | bytes 30932992 | tf_op jit(solution)/shard_map/dot_general | solution.py:51
  117.4 0.0 reduce-scatter.3.cloned.1.call-update
  117.5 0.0 all-gather.4.cloned.1.call-start
  117.5 0.6 copy-done.7
  118.1 0.3 copy-done.6
  118.4 0.1 copy.14
  118.6 0.1 convert_reduce_fusion
  118.6 87.5 %reduce-scatter.3.cloned.1.call-done = f32[512,256]{0,1:T(8,128)} async-done(((f32[4096,256]{0,1:T(8,128)}), f32[512,256]{0,1:T(8,128)}) %reduce-scatter.3.cloned.1.call-update) | async-done | bytes 524304 | tf_op jit(solution)/shard_map/reduce_scatter | solution.py:50
  206.1 1.9 multiply_reduce_fusion
  208.0 20.8 %all-reduce = (f32[]{:T(128)}, f32[]{:T(128)}) all-reduce(f32[]{:T(128)} %get-tuple-element.4, f32[]{:T(128)} %get-tuple-element.3), channel_id=1, replica_groups=mesh['layer'=4,'lat'=8] {'lat'}, use_global_device_ids=true, to_apply=%region_3.4 | all-reduce | flops 2 | bytes 16 | tf_op jit(solution)/shard_map/psum | solution.py:61
  229.5 1.9 divide_convert_fusion
  231.3 0.0 all-gather.4.cloned.1.call-update
  231.3 0.2 reduce-scatter.5.cloned.1.call-start
  231.6 48.2 %all-gather.4.cloned.1.call-done = bf16[4096,256]{0,1:T(8,128)(2,1)} async-done(((bf16[512,256]{0,1:T(8,128)(2,1)}), bf16[4096,256]{0,1:T(8,128)(2,1)}) %all-gather.4.cloned.1.call-update) | async-done | bytes 2097168 | tf_op jit(solution)/shard_map/all_gather | solution.py:68
  279.8 12.2 %convolution_bitcast_fusion.1 = f32[3072,256]{0,1:T(8,128)S(1)} fusion(bf16[4096,256]{0,1:T(8,128)(2,1)} %all-gather.4.cloned.1.call-done, bf16[3072,4096]{1,0:T(8,128)(2,1)} %bitcast.76), kind=kOutput, calls=%fused_computation.6 | convolution fusion | flops 6442450944 | bytes 30408704 | tf_op jit(solution)/shard_map/dot_general | solution.py:69
  292.0 2.4 copy.15
  294.4 2.4 copy.16
  296.8 2.0 broadcast_multiply_fusion
  298.8 0.0 reduce-scatter.5.cloned.1.call-update
  299.6 6.7 %psum.23 = f32[]{:T(128)} all-reduce(f32[]{:T(128)S(6)} %div.23), channel_id=1, replica_groups=mesh['layer'=4,'lat'=8] {'layer'}, use_global_device_ids=true, to_apply=%region_7.8 | all-reduce | flops 1 | bytes 8 | tf_op jit(solution)/shard_map/psum | solution.py:66
  306.2 14.2 %convolution_convert_fusion = bf16[3072,4096]{1,0:T(8,128)(2,1)} fusion(bf16[3072,256]{0,1:T(8,128)(2,1)S(1)} %bitcast.70, bf16[4096,256]{0,1:T(8,128)(2,1)} %all-gather.4.cloned.1.call-done), kind=kOutput, calls=%fused_computation | convolution fusion | flops 6455033856 | bytes 28835840 | tf_op jit(solution)/shard_map/dot_general | solution.py:73
  320.4 14.7 %reduce-scatter.5.cloned.1.call-done = f32[1,768,256]{1,2,0:T(8,128)} async-done(((f32[4,768,256]{1,2,0:T(8,128)}), f32[1,768,256]{1,2,0:T(8,128)}) %reduce-scatter.5.cloned.1.call-update) | async-done | bytes 786448 | tf_op jit(solution)/shard_map/reduce_scatter | solution.py:77
  335.1 6.4 %fusion.2 = bf16[1,768,4096]{2,1,0:T(8,128)(2,1)} fusion(bf16[8192,256]{1,0:T(8,128)(2,1)} %copy-done.4, s32[]{:T(128)S(6)} %select_n.18, f32[1,768,256]{1,2,0:T(8,128)} %reduce-scatter.5.cloned.1.call-done, s32[1,768,256]{1,2,0:T(8,128)S(1)} %copy-done.3), kind=kOutput, calls=%fused_computation.4 | convolution fusion | flops 1614348288 | bytes 9961476 | tf_op jit(solution)/shard_map/dot_general | solution.py:79
  (38 shorter events, 0.4 us)
Async XLA Ops:
  7.2 69.2 %copy-start.5 = (bf16[1,512,256]{2,1,0:T(8,128)(2,1)S(1)}, bf16[1,512,256]{2,1,0:T(8,128)(2,1)}, u32[]{:S(2)}) copy-start(bf16[1,512,256]{2,1,0:T(8,128)(2,1)} %param.8) | copy-start | bytes 786436
  7.2 91.2 %all-gather.6.cloned.1.call-start = ((), (), s32[]{:S(2)}) async-start(), calls=%async_computation.5 | async-start | bytes 1966080 | tf_op jit(solution)/shard_map/all_gather | solution.py:41
  7.2 12.6 %collective-permute-start = (bf16[512,256]{1,0:T(8,128)(2,1)}, bf16[512,256]{1,0:T(8,128)(2,1)S(1)}, u32[]{:S(2)}, u32[]{:S(2)}) collective-permute-start(bf16[512,256]{1,0:T(8,128)(2,1)} %bitcast.72), channel_id=1, source_target_pairs={{0,1},{1,2},{2,3},{3,4},{4,5},{5,6},{6,7},{7,0},{8,9},{9,10},{10,1... | collective-permute-start | bytes 786440 | tf_op jit(solution)/shard_map/ppermute | solution.py:21
  19.8 10.2 %collective-permute-start.1 = (bf16[512,256]{1,0:T(8,128)(2,1)S(1)}, bf16[512,256]{1,0:T(8,128)(2,1)S(1)}, u32[]{:S(2)}, u32[]{:S(2)}) collective-permute-start(bf16[512,256]{1,0:T(8,128)(2,1)S(1)} %collective-permute-done), channel_id=1, source_target_pairs={{0,1},{1,2},{2,3},{3,4},{4,5},{5,6},{6,7},{7,0},{8,9},{9,10},{10,1... | collective-permute-start | bytes 786440 | tf_op jit(solution)/shard_map/ppermute | solution.py:21
  30.0 9.3 %collective-permute-start.2 = (bf16[512,256]{1,0:T(8,128)(2,1)S(1)}, bf16[512,256]{1,0:T(8,128)(2,1)S(1)}, u32[]{:S(2)}, u32[]{:S(2)}) collective-permute-start(bf16[512,256]{1,0:T(8,128)(2,1)S(1)} %collective-permute-done.1), channel_id=1, source_target_pairs={{0,1},{1,2},{2,3},{3,4},{4,5},{5,6},{6,7},{7,0},{8,9},{9,10},{10,1... | collective-permute-start | bytes 786440 | tf_op jit(solution)/shard_map/ppermute | solution.py:21
  39.3 9.1 %collective-permute-start.3 = (bf16[512,256]{1,0:T(8,128)(2,1)S(1)}, bf16[512,256]{1,0:T(8,128)(2,1)S(1)}, u32[]{:S(2)}, u32[]{:S(2)}) collective-permute-start(bf16[512,256]{1,0:T(8,128)(2,1)S(1)} %collective-permute-done.2), channel_id=1, source_target_pairs={{0,1},{1,2},{2,3},{3,4},{4,5},{5,6},{6,7},{7,0},{8,9},{9,10},{10,1... | collective-permute-start | bytes 786440 | tf_op jit(solution)/shard_map/ppermute | solution.py:21
  48.3 9.1 %collective-permute-start.4 = (bf16[512,256]{1,0:T(8,128)(2,1)S(1)}, bf16[512,256]{1,0:T(8,128)(2,1)S(1)}, u32[]{:S(2)}, u32[]{:S(2)}) collective-permute-start(bf16[512,256]{1,0:T(8,128)(2,1)S(1)} %collective-permute-done.3), channel_id=1, source_target_pairs={{0,1},{1,2},{2,3},{3,4},{4,5},{5,6},{6,7},{7,0},{8,9},{9,10},{10,1... | collective-permute-start | bytes 786440 | tf_op jit(solution)/shard_map/ppermute | solution.py:21
  57.4 9.7 %collective-permute-start.5 = (bf16[512,256]{1,0:T(8,128)(2,1)S(1)}, bf16[512,256]{1,0:T(8,128)(2,1)S(1)}, u32[]{:S(2)}, u32[]{:S(2)}) collective-permute-start(bf16[512,256]{1,0:T(8,128)(2,1)S(1)} %collective-permute-done.4), channel_id=1, source_target_pairs={{0,1},{1,2},{2,3},{3,4},{4,5},{5,6},{6,7},{7,0},{8,9},{9,10},{10,1... | collective-permute-start | bytes 786440 | tf_op jit(solution)/shard_map/ppermute | solution.py:21
  67.1 9.1 %collective-permute-start.6 = (bf16[512,256]{1,0:T(8,128)(2,1)S(1)}, bf16[512,256]{1,0:T(8,128)(2,1)S(1)}, u32[]{:S(2)}, u32[]{:S(2)}) collective-permute-start(bf16[512,256]{1,0:T(8,128)(2,1)S(1)} %collective-permute-done.5), channel_id=1, source_target_pairs={{0,1},{1,2},{2,3},{3,4},{4,5},{5,6},{6,7},{7,0},{8,9},{9,10},{10,1... | collective-permute-start | bytes 786440 | tf_op jit(solution)/shard_map/ppermute | solution.py:21
  68.5 8.1 %copy-start.2 = (s32[1,768,256]{1,2,0:T(8,128)}, s32[1,768,256]{1,2,0:T(8,128)S(1)}, u32[]{:S(2)}) copy-start(s32[1,768,256]{1,2,0:T(8,128)S(1)} %copy.13) | copy-start | bytes 2359300
  69.3 9.3 %copy-start.9 = (bf16[1,768,4096]{2,1,0:T(8,128)(2,1)S(1)}, bf16[1,768,4096]{2,1,0:T(8,128)(2,1)}, u32[]{:S(2)}) copy-start(bf16[1,768,4096]{2,1,0:T(8,128)(2,1)} %param.12) | copy-start | bytes 18874372
  76.6 1.9 copy-start.4
  81.3 124.8 %reduce-scatter.3.cloned.1.call-start = ((), (), s32[]{:S(2)}) async-start(), calls=%async_computation.2 | async-start | bytes 4718592 | tf_op jit(solution)/shard_map/reduce_scatter | solution.py:50
  102.7 1.1 copy-start
  117.4 0.7 copy-start.7
  117.4 1.0 copy-start.6
  117.4 1.2 copy-start.8
  117.5 162.3 %all-gather.4.cloned.1.call-start = ((), (), s32[]{:S(2)}) async-start(), calls=%async_computation.3 | async-start | bytes 2359296 | tf_op jit(solution)/shard_map/all_gather | solution.py:68
  231.3 103.7 %reduce-scatter.5.cloned.1.call-start = ((), (), s32[]{:S(2)}) async-start(), calls=%async_computation.4 | async-start | bytes 3932160 | tf_op jit(solution)/shard_map/reduce_scatter | solution.py:77
  298.8 7.5 %copy-start.1 = (bf16[32,8,4,768]{3,1,2,0:T(8,128)(2,1)S(1)}, bf16[32,8,4,768]{3,1,2,0:T(8,128)(2,1)}, u32[]{:S(2)}) copy-start(bf16[32,8,4,768]{3,1,2,0:T(8,128)(2,1)} %copy-done) | copy-start | bytes 4718596
  306.2 28.9 %copy-start.3 = (s32[1,768,256]{1,2,0:T(8,128)S(1)}, s32[1,768,256]{1,2,0:T(8,128)}, u32[]{:S(2)}) copy-start(s32[1,768,256]{1,2,0:T(8,128)} %copy-done.2) | copy-start | bytes 2359300
Sparse Core Ops, SparseCore 0:
  81.4 16.9 all-gather.5
  117.6 88.4 reduce-scatter.2
  231.5 48.2 all-gather.3
  298.9 36.1 reduce-scatter.4
